TPU v7x, 32 devices: a whole 2x2x4 slice. The times are simulated.
32 devices in a mesh: row: 16 (over z, y, core), col: 2 (over x).
Axes of the slice: x: 2, y: 2, z: 4, core: 2. Of those that a mesh axis runs over, the one named last changes fastest.
Arguments:
- residues: int32 [512], P('row'), may hold values from 0 to 20
- embed_table: bfloat16 [21, 256], replicated, may hold values from -6 to 6
- conv_first: bfloat16 [4352, 256], replicated, may hold values from -0.09375 to 0.09375
- conv_second: bfloat16 [4352, 256], replicated, may hold values from -0.09375 to 0.09375
- proj_row: bfloat16 [256, 64], replicated, may hold values from -0.375 to 0.375
- proj_col: bfloat16 [256, 64], replicated, may hold values from -0.375 to 0.375
- pair_weights: bfloat16 [4, 64, 576], replicated, may hold values from -0.25 to 0.25
Outputs:
- pair_out: bfloat16 [64, 512, 512], P(None, 'row', 'col')
All inputs are finite; a program needn't handle non-finite values.
Results may differ from a plain program's by a relative error of at most 0.018.
Values may be sent and summed in bfloat16 or wider, within the bound.
A program may use at most 64 MiB of HBM per device.

v0:
```python
import jax
import jax.numpy as jnp
from jax import lax
from jax.sharding import PartitionSpec as P

KERNEL = 17
LAYERS = 4


def padded_2(shard, sides, width):
    for axis, dim in sides:
        size, length = (lax.axis_size(axis), shard.shape[dim])
        up = [(i, (i + 1) % size) for i in range(size - 1)]
        down = [(j, i) for i, j in up]
        last = lax.slice_in_dim(shard, length - width, length, axis=dim)
        leading = lax.slice_in_dim(shard, 0, width, axis=dim)
        before = lax.ppermute(last, axis, up)
        after = lax.ppermute(leading, axis, down)
        shard = jnp.concatenate([before, shard, after], axis=dim)
    return shard


def elu(v):
    return jnp.where(v > 0, v, jnp.expm1(jnp.minimum(v, 0.0)))


def conv_seq(feats, weight_stack):
    half = KERNEL // 2
    length = feats.shape[0]
    padded = padded_2(feats, (("row", 0),), half)
    windows = jnp.concatenate([padded[k : k + length] for k in range(KERNEL)], axis=1)
    return jnp.dot(windows, weight_stack, preferred_element_type=jnp.float32)


def offset_sum(weight_stack, activation_map, dilation_rate, row_span, column_span):
    chans = activation_map.shape[0]
    total = jnp.zeros((weight_stack.shape[0], row_span, column_span), jnp.float32)
    for offset_row in range(3):
        for offset_column in range(3):
            tap = 3 * offset_row + offset_column
            block = weight_stack[:, tap * chans : (tap + 1) * chans]
            window_extent = activation_map[
                :,
                offset_row * dilation_rate : offset_row * dilation_rate + row_span,
                offset_column * dilation_rate : offset_column * dilation_rate + column_span,
            ]
            total = total + jnp.einsum(
                "oc,cij->oij", block, window_extent, preferred_element_type=jnp.float32
            )
    return total


def apply_activation(pair_features):
    return elu(pair_features.astype(jnp.float32)).astype(jnp.bfloat16)


def layer_borders(pair_features, weight_stack, dilation_rate):
    activation_map = padded_2(
        apply_activation(pair_features), (("row", 1), ("col", 2)), dilation_rate
    )
    output_map = offset_sum(
        weight_stack, activation_map, dilation_rate, pair_features.shape[1], pair_features.shape[2]
    )
    return (pair_features.astype(jnp.float32) + output_map).astype(jnp.bfloat16)


def local(residues, embed_table, conv_first, conv_second, proj_row, proj_col, pair_weights):
    row_span = residues.shape[0]
    window_extent = row_span * lax.axis_size("row")
    tile = window_extent // lax.axis_size("col")
    col_start = lax.axis_index("col") * tile
    onehot = (
        residues[:, None] == jnp.arange(embed_table.shape[0], dtype=jnp.int32)[None, :]
    ).astype(jnp.bfloat16)
    embedded = jnp.dot(onehot, embed_table, preferred_element_type=jnp.float32).astype(jnp.bfloat16)
    first = elu(conv_seq(embedded, conv_first)).astype(jnp.bfloat16)
    second = (first.astype(jnp.float32) + elu(conv_seq(first, conv_second))).astype(jnp.bfloat16)
    left = jnp.dot(second, proj_row, preferred_element_type=jnp.float32).astype(jnp.bfloat16)
    local_right = jnp.dot(second, proj_col, preferred_element_type=jnp.float32).astype(jnp.bfloat16)
    every_right = lax.all_gather(local_right, "row", axis=0, tiled=True)
    right = lax.dynamic_slice_in_dim(every_right, col_start, tile, 0)
    pair_features = (
        left.T.astype(jnp.float32)[:, :, None] + right.T.astype(jnp.float32)[:, None, :]
    ).astype(jnp.bfloat16)
    for layer_number in range(LAYERS):
        pair_features = layer_borders(pair_features, pair_weights[layer_number], 2**layer_number)
    return pair_features


def solution(mesh):
    return jax.shard_map(
        local,
        mesh=mesh,
        in_specs=(P("row"), P(), P(), P(), P(), P(), P()),
        out_specs=P(None, "row", "col"),
        check_vma=False,
    )
```

profile of v0, /device:TPU:7, one launch (start us, length us, event | category | flops | bytes accessed | tf_op | source)
XLA Modules:
  0.0 166.0 jit_solution(4269461075004953706)
XLA Ops:
  1.1 3.7 %collective-permute-start = (bf16[8,256]{1,0:T(8,128)(2,1)S(1)}, bf16[8,256]{1,0:T(8,128)(2,1)S(1)}, u32[]{:S(2)}, u32[]{:S(2)}) collective-permute-start(bf16[8,256]{1,0:T(8,128)(2,1)S(1)} %get-tuple-element.36), channel_id=1, source_target_pairs={{0,2},{2,4},{4,6},{6,8},{8,10},{10,12},{12,14},{14,16},{16,18},{18... | collective-permute-start | bytes 12296 | tf_op jit(solution)/shard_map/ppermute | solution.py:17
  6.9 3.7 %collective-permute-done.1 = bf16[8,256]{1,0:T(8,128)(2,1)S(1)} collective-permute-done((bf16[8,256]{1,0:T(8,128)(2,1)S(1)}, bf16[8,256]{1,0:T(8,128)(2,1)S(1)}, u32[]{:S(2)}, u32[]{:S(2)}) %collective-permute-start.1) | collective-permute-done | bytes 4128 | tf_op jit(solution)/shard_map/ppermute | solution.py:18
  14.0 2.4 %collective-permute-start.3 = (bf16[8,256]{1,0:T(8,128)(2,1)S(1)}, bf16[8,256]{1,0:T(8,128)(2,1)S(1)}, u32[]{:S(2)}, u32[]{:S(2)}) collective-permute-start(bf16[8,256]{1,0:T(8,128)(2,1)S(1)} %get-tuple-element.33), channel_id=1, source_target_pairs={{2,0},{4,2},{6,4},{8,6},{10,8},{12,10},{14,12},{16,14},{18,16},{20... | collective-permute-start | bytes 12296 | tf_op jit(solution)/shard_map/ppermute | solution.py:18
  16.5 3.3 %collective-permute-done.3 = bf16[8,256]{1,0:T(8,128)(2,1)S(1)} collective-permute-done((bf16[8,256]{1,0:T(8,128)(2,1)S(1)}, bf16[8,256]{1,0:T(8,128)(2,1)S(1)}, u32[]{:S(2)}, u32[]{:S(2)}) %collective-permute-start.3) | collective-permute-done | bytes 4128 | tf_op jit(solution)/shard_map/ppermute | solution.py:18
  22.3 17.0 %all_gather.3 = bf16[512,64]{1,0:T(8,128)(2,1)S(1)} all-gather(bf16[32,64]{1,0:T(8,128)(2,1)S(1)} %convolution_convert_fusion.1), channel_id=1, replica_groups=mesh['row'=16,'col'=2] {'row'}, dimensions={0}, use_global_device_ids=true | all-gather | bytes 69632 | tf_op jit(solution)/shard_map/all_gather | solution.py:80
  40.4 2.3 %collective-permute-start.4 = (bf16[64,1,256]{2,0,1:T(8,128)(2,1)S(1)}, bf16[64,1,256]{2,0,1:T(8,128)(2,1)S(1)}, u32[]{:S(2)}, u32[]{:S(2)}) collective-permute-start(bf16[64,1,256]{2,0,1:T(8,128)(2,1)S(1)} %get-tuple-element.27), channel_id=1, source_target_pairs={{0,2},{2,4},{4,6},{6,8},{8,10},{10,12},{12,14},{14,16},{16,18},{18... | collective-permute-start | bytes 98312 | tf_op jit(solution)/shard_map/ppermute | solution.py:17
  44.7 2.6 %fusion.86 = f32[32,256,64]{1,2,0:T(8,128)} fusion(f32[64,256]{1,0:T(8,128)S(1)} %copy.10, f32[64,32]{0,1:T(8,128)S(1)} %fusion.13, bf16[64,576]{1,0:T(8,128)(2,1)S(1)} %get-tuple-element.31), kind=kOutput, calls=%fused_computation.115 | convolution fusion | flops 70778880 | bytes 2195456 | tf_op jit(solution)/shard_map/oc,cij->oij/dot_general | solution.py:47
  51.2 4.0 %collective-permute-start.7 = (bf16[64,34,1]{0,1,2:T(8,128)(2,1)S(1)}, bf16[64,34,1]{0,1,2:T(8,128)(2,1)S(1)}, u32[]{:S(2)}, u32[]{:S(2)}) collective-permute-start(bf16[64,34,1]{0,1,2:T(8,128)(2,1)S(1)} %copy.13), channel_id=1, source_target_pairs={{1,0},{3,2},{5,4},{7,6},{9,8},{11,10},{13,12},{15,14},{17,16},{19,... | collective-permute-start | bytes 13064 | tf_op jit(solution)/shard_map/ppermute | solution.py:18
  55.2 2.6 %fusion.72 = f32[32,256,64]{1,2,0:T(8,128)} fusion(bf16[64,1,256]{2,0,1:T(8,128)(2,1)S(1)} %collective-permute-done.5, bf16[64,32,256]{2,0,1:T(8,128)(2,1)S(1)} %fusion.8, bf16[64,576]{1,0:T(8,128)(2,1)} %copy-done.19), kind=kOutput, calls=%fused_computation.99 | convolution fusion | flops 69206016 | bytes 3194880 | tf_op jit(solution)/shard_map/oc,cij->oij/dot_general | solution.py:47
  57.8 2.6 %fusion.82 = f32[32,256,64]{1,2,0:T(8,128)} fusion(bf16[64,32,256]{2,0,1:T(8,128)(2,1)S(1)} %fusion.8, bf16[64,1,256]{2,0,1:T(8,128)(2,1)S(1)} %collective-permute-done.4, bf16[64,576]{1,0:T(8,128)(2,1)} %copy-done.19), kind=kOutput, calls=%fused_computation.110 | convolution fusion | flops 69206016 | bytes 3194880 | tf_op jit(solution)/shard_map/oc,cij->oij/dot_general | solution.py:47
  69.2 3.5 %collective-permute-start.8 = (bf16[64,2,256]{2,0,1:T(8,128)(2,1)S(1)}, bf16[64,2,256]{2,0,1:T(8,128)(2,1)S(1)}, u32[]{:S(2)}, u32[]{:S(2)}) collective-permute-start(bf16[64,2,256]{2,0,1:T(8,128)(2,1)S(1)} %get-tuple-element.25), channel_id=1, source_target_pairs={{0,2},{2,4},{4,6},{6,8},{8,10},{10,12},{12,14},{14,16},{16,18},{18... | collective-permute-start | bytes 196616 | tf_op jit(solution)/shard_map/ppermute | solution.py:17
  74.6 2.5 %fusion.121 = f32[32,256,64]{1,2,0:T(8,128)} fusion(bf16[64,576]{1,0:T(8,128)(2,1)S(1)} %copy-done.17, bf16[64,32,256]{2,0,1:T(8,128)(2,1)S(1)} %get-tuple-element.38), kind=kOutput, calls=%fused_computation.268 | convolution fusion | flops 69730304 | bytes 3162112 | tf_op jit(solution)/shard_map/oc,cij->oij/dot_general | solution.py:47
  82.3 4.2 %collective-permute-start.11 = (bf16[64,36,2]{0,2,1:T(2,128)(2,1)}, bf16[64,36,2]{0,2,1:T(2,128)(2,1)S(1)}, u32[]{:S(2)}, u32[]{:S(2)}) collective-permute-start(bf16[64,36,2]{0,2,1:T(2,128)(2,1)} %copy.17), channel_id=1, source_target_pairs={{1,0},{3,2},{5,4},{7,6},{9,8},{11,10},{13,12},{15,14},{17,16},{19,... | collective-permute-start | bytes 27656 | tf_op jit(solution)/shard_map/ppermute | solution.py:18
  86.5 2.7 %fusion.54 = f32[32,256,64]{1,2,0:T(8,128)} fusion(bf16[64,2,256]{2,0,1:T(8,128)(2,1)} %copy-done.18, bf16[64,32,256]{2,0,1:T(8,128)(2,1)S(1)} %get-tuple-element.37, bf16[64,576]{1,0:T(8,128)(2,1)S(1)} %copy-done.17), kind=kOutput, calls=%fused_computation.81 | convolution fusion | flops 69206016 | bytes 3227648 | tf_op jit(solution)/shard_map/oc,cij->oij/dot_general | solution.py:47
  91.7 2.4 %pad_maximum_fusion.2 = (bf16[64,36,258]{2,0,1:T(8,128)(2,1)S(1)}, bf16[64,36,258]{2,0,1:T(8,128)(2,1)S(1)}) fusion(bf16[64,36,2]{2,0,1:T(8,128)(2,1)S(1)} %copy.18, bf16[64,2,256]{2,0,1:T(8,128)(2,1)} %copy-done.18, bf16[64,32,256]{2,0,1:T(8,128)(2,1)S(1)} %get-tuple-element.37, bf16[64,2,256]{2,0,1:T(8,128)(2,1)S(1)} %collective-permute-done.8, ...), kind=kLoop, calls=%fused_computation.30 | loop fusion | flops 9510912 | bytes 3575808 | tf_op jit(solution)/shard_map/concatenate | solution.py:19
  100.6 3.1 %collective-permute-start.12 = (bf16[64,4,256]{2,0,1:T(8,128)(2,1)S(1)}, bf16[64,4,256]{2,0,1:T(8,128)(2,1)S(1)}, u32[]{:S(2)}, u32[]{:S(2)}) collective-permute-start(bf16[64,4,256]{2,0,1:T(8,128)(2,1)S(1)} %get-tuple-element.23), channel_id=1, source_target_pairs={{0,2},{2,4},{4,6},{6,8},{8,10},{10,12},{12,14},{14,16},{16,18},{18... | collective-permute-start | bytes 393224 | tf_op jit(solution)/shard_map/ppermute | solution.py:17
  105.6 2.5 %fusion.120 = f32[32,256,64]{1,2,0:T(8,128)} fusion(bf16[64,576]{1,0:T(8,128)(2,1)S(1)} %copy-done.16, bf16[64,32,256]{2,0,1:T(8,128)(2,1)S(1)} %get-tuple-element.40), kind=kOutput, calls=%fused_computation.258 | convolution fusion | flops 69730304 | bytes 3162112 | tf_op jit(solution)/shard_map/oc,cij->oij/dot_general | solution.py:47
  108.2 2.7 %collective-permute-done.13 = bf16[64,4,256]{2,0,1:T(8,128)(2,1)S(1)} collective-permute-done((bf16[64,4,256]{2,0,1:T(8,128)(2,1)S(1)}, bf16[64,4,256]{2,0,1:T(8,128)(2,1)S(1)}, u32[]{:S(2)}, u32[]{:S(2)}) %collective-permute-start.13) | collective-permute-done | bytes 131104 | tf_op jit(solution)/shard_map/ppermute | solution.py:18
  115.3 4.2 %collective-permute-start.15 = (bf16[64,40,4]{0,1,2:T(8,128)(2,1)S(1)}, bf16[64,40,4]{0,1,2:T(8,128)(2,1)S(1)}, u32[]{:S(2)}, u32[]{:S(2)}) collective-permute-start(bf16[64,40,4]{0,1,2:T(8,128)(2,1)S(1)} %copy.21), channel_id=1, source_target_pairs={{1,0},{3,2},{5,4},{7,6},{9,8},{11,10},{13,12},{15,14},{17,16},{19,... | collective-permute-start | bytes 61448 | tf_op jit(solution)/shard_map/ppermute | solution.py:18
  124.7 2.6 %pad_maximum_fusion.1 = (bf16[64,40,260]{2,0,1:T(8,128)(2,1)S(1)}, bf16[64,40,260]{2,0,1:T(8,128)(2,1)S(1)}) fusion(bf16[64,40,4]{2,0,1:T(8,128)(2,1)S(1)} %copy.22, bf16[64,4,256]{2,0,1:T(8,128)(2,1)S(1)} %collective-permute-done.13, bf16[64,32,256]{2,0,1:T(8,128)(2,1)S(1)} %get-tuple-element.39, bf16[64,4,256]{2,0,1:T(8,128)(2,1)S(1)} %collective-permute-done.12, ...), kind=kLoop, calls=%fused_computation.28 | loop fusion | flops 10649600 | bytes 4014080 | tf_op jit(solution)/shard_map/concatenate | solution.py:19
  133.9 2.4 %collective-permute-start.16 = (bf16[64,8,256]{2,0,1:T(8,128)(2,1)S(1)}, bf16[64,8,256]{2,0,1:T(8,128)(2,1)S(1)}, u32[]{:S(2)}, u32[]{:S(2)}) collective-permute-start(bf16[64,8,256]{2,0,1:T(8,128)(2,1)S(1)} %get-tuple-element.21), channel_id=1, source_target_pairs={{0,2},{2,4},{4,6},{6,8},{8,10},{10,12},{12,14},{14,16},{16,18},{18... | collective-permute-start | bytes 786440 | tf_op jit(solution)/shard_map/ppermute | solution.py:17
  138.3 2.5 %fusion.119 = f32[32,256,64]{1,2,0:T(8,128)} fusion(bf16[64,576]{1,0:T(8,128)(2,1)S(1)} %get-tuple-element.29, bf16[64,32,256]{2,0,1:T(8,128)(2,1)S(1)} %get-tuple-element.42), kind=kOutput, calls=%fused_computation.248 | convolution fusion | flops 69730304 | bytes 3162112 | tf_op jit(solution)/shard_map/oc,cij->oij/dot_general | solution.py:47
  140.8 4.1 %collective-permute-done.17 = bf16[64,8,256]{2,0,1:T(8,128)(2,1)S(1)} collective-permute-done((bf16[64,8,256]{2,0,1:T(8,128)(2,1)S(1)}, bf16[64,8,256]{2,0,1:T(8,128)(2,1)S(1)}, u32[]{:S(2)}, u32[]{:S(2)}) %collective-permute-start.17) | collective-permute-done | bytes 262176 | tf_op jit(solution)/shard_map/ppermute | solution.py:18
  148.0 4.3 %collective-permute-start.19 = (bf16[64,48,8]{0,2,1:T(8,128)(2,1)}, bf16[64,48,8]{0,2,1:T(8,128)(2,1)S(1)}, u32[]{:S(2)}, u32[]{:S(2)}) collective-permute-start(bf16[64,48,8]{0,2,1:T(8,128)(2,1)} %copy.25), channel_id=1, source_target_pairs={{1,0},{3,2},{5,4},{7,6},{9,8},{11,10},{13,12},{15,14},{17,16},{19,... | collective-permute-start | bytes 147464 | tf_op jit(solution)/shard_map/ppermute | solution.py:18
  (179 shorter events, 77.1 us)
Async XLA Ops:
  0.0 13.3 %copy-start.21 = (bf16[4,64,576]{2,1,0:T(8,128)(2,1)S(1)}, bf16[4,64,576]{2,1,0:T(8,128)(2,1)}, u32[]{:S(2)}) copy-start(bf16[4,64,576]{2,1,0:T(8,128)(2,1)} %param.13) | copy-start | bytes 884740
  1.1 5.6 %collective-permute-start = (bf16[8,256]{1,0:T(8,128)(2,1)S(1)}, bf16[8,256]{1,0:T(8,128)(2,1)S(1)}, u32[]{:S(2)}, u32[]{:S(2)}) collective-permute-start(bf16[8,256]{1,0:T(8,128)(2,1)S(1)} %get-tuple-element.36), channel_id=1, source_target_pairs={{0,2},{2,4},{4,6},{6,8},{8,10},{10,12},{12,14},{14,16},{16,18},{18... | collective-permute-start | bytes 12296 | tf_op jit(solution)/shard_map/ppermute | solution.py:17
  4.8 5.8 %collective-permute-start.1 = (bf16[8,256]{1,0:T(8,128)(2,1)S(1)}, bf16[8,256]{1,0:T(8,128)(2,1)S(1)}, u32[]{:S(2)}, u32[]{:S(2)}) collective-permute-start(bf16[8,256]{1,0:T(8,128)(2,1)S(1)} %get-tuple-element.35), channel_id=1, source_target_pairs={{2,0},{4,2},{6,4},{8,6},{10,8},{12,10},{14,12},{16,14},{18,16},{20... | collective-permute-start | bytes 12296 | tf_op jit(solution)/shard_map/ppermute | solution.py:18
  11.3 10.7 %copy-start.23 = (bf16[256,64]{0,1:T(8,128)(2,1)S(1)}, bf16[256,64]{0,1:T(8,128)(2,1)}, u32[]{:S(2)}) copy-start(bf16[256,64]{0,1:T(8,128)(2,1)} %param.12) | copy-start | bytes 98308
  11.3 10.9 %copy-start.22 = (bf16[256,64]{0,1:T(8,128)(2,1)S(1)}, bf16[256,64]{0,1:T(8,128)(2,1)}, u32[]{:S(2)}) copy-start(bf16[256,64]{0,1:T(8,128)(2,1)} %param.11) | copy-start | bytes 98308
  11.3 5.0 %collective-permute-start.2 = (bf16[8,256]{1,0:T(8,128)(2,1)S(1)}, bf16[8,256]{1,0:T(8,128)(2,1)S(1)}, u32[]{:S(2)}, u32[]{:S(2)}) collective-permute-start(bf16[8,256]{1,0:T(8,128)(2,1)S(1)} %get-tuple-element.34), channel_id=1, source_target_pairs={{0,2},{2,4},{4,6},{6,8},{8,10},{10,12},{12,14},{14,16},{16,18},{18... | collective-permute-start | bytes 12296 | tf_op jit(solution)/shard_map/ppermute | solution.py:17
  14.0 30.8 %copy-start.19 = (bf16[64,576]{1,0:T(8,128)(2,1)}, bf16[64,576]{1,0:T(8,128)(2,1)S(1)}, u32[]{:S(2)}) copy-start(bf16[64,576]{1,0:T(8,128)(2,1)S(1)} %get-tuple-element.31) | copy-start | bytes 221188
  14.0 5.8 %collective-permute-start.3 = (bf16[8,256]{1,0:T(8,128)(2,1)S(1)}, bf16[8,256]{1,0:T(8,128)(2,1)S(1)}, u32[]{:S(2)}, u32[]{:S(2)}) collective-permute-start(bf16[8,256]{1,0:T(8,128)(2,1)S(1)} %get-tuple-element.33), channel_id=1, source_target_pairs={{2,0},{4,2},{6,4},{8,6},{10,8},{12,10},{14,12},{16,14},{18,16},{20... | collective-permute-start | bytes 12296 | tf_op jit(solution)/shard_map/ppermute | solution.py:18
  40.4 7.0 %collective-permute-start.4 = (bf16[64,1,256]{2,0,1:T(8,128)(2,1)S(1)}, bf16[64,1,256]{2,0,1:T(8,128)(2,1)S(1)}, u32[]{:S(2)}, u32[]{:S(2)}) collective-permute-start(bf16[64,1,256]{2,0,1:T(8,128)(2,1)S(1)} %get-tuple-element.27), channel_id=1, source_target_pairs={{0,2},{2,4},{4,6},{6,8},{8,10},{10,12},{12,14},{14,16},{16,18},{18... | collective-permute-start | bytes 98312 | tf_op jit(solution)/shard_map/ppermute | solution.py:17
  42.7 6.1 %collective-permute-start.5 = (bf16[64,1,256]{2,0,1:T(8,128)(2,1)S(1)}, bf16[64,1,256]{2,0,1:T(8,128)(2,1)S(1)}, u32[]{:S(2)}, u32[]{:S(2)}) collective-permute-start(bf16[64,1,256]{2,0,1:T(8,128)(2,1)S(1)} %get-tuple-element.28), channel_id=1, source_target_pairs={{2,0},{4,2},{6,4},{8,6},{10,8},{12,10},{14,12},{16,14},{18,16},{20... | collective-permute-start | bytes 98312 | tf_op jit(solution)/shard_map/ppermute | solution.py:18
  49.9 10.8 %collective-permute-start.6 = (bf16[64,34,1]{0,1,2:T(8,128)(2,1)S(1)}, bf16[64,34,1]{0,1,2:T(8,128)(2,1)S(1)}, u32[]{:S(2)}, u32[]{:S(2)}) collective-permute-start(bf16[64,34,1]{0,1,2:T(8,128)(2,1)S(1)} %copy.11), channel_id=1, source_target_pairs={{0,1},{2,3},{4,5},{6,7},{8,9},{10,11},{12,13},{14,15},{16,17},{18,... | collective-permute-start | bytes 13064 | tf_op jit(solution)/shard_map/ppermute | solution.py:17
  51.2 9.1 %collective-permute-start.7 = (bf16[64,34,1]{0,1,2:T(8,128)(2,1)S(1)}, bf16[64,34,1]{0,1,2:T(8,128)(2,1)S(1)}, u32[]{:S(2)}, u32[]{:S(2)}) collective-permute-start(bf16[64,34,1]{0,1,2:T(8,128)(2,1)S(1)} %copy.13), channel_id=1, source_target_pairs={{1,0},{3,2},{5,4},{7,6},{9,8},{11,10},{13,12},{15,14},{17,16},{19,... | collective-permute-start | bytes 13064 | tf_op jit(solution)/shard_map/ppermute | solution.py:18
  69.2 8.0 %collective-permute-start.8 = (bf16[64,2,256]{2,0,1:T(8,128)(2,1)S(1)}, bf16[64,2,256]{2,0,1:T(8,128)(2,1)S(1)}, u32[]{:S(2)}, u32[]{:S(2)}) collective-permute-start(bf16[64,2,256]{2,0,1:T(8,128)(2,1)S(1)} %get-tuple-element.25), channel_id=1, source_target_pairs={{0,2},{2,4},{4,6},{6,8},{8,10},{10,12},{12,14},{14,16},{16,18},{18... | collective-permute-start | bytes 196616 | tf_op jit(solution)/shard_map/ppermute | solution.py:17
  72.7 6.5 %collective-permute-start.9 = (bf16[64,2,256]{2,0,1:T(8,128)(2,1)S(1)}, bf16[64,2,256]{2,0,1:T(8,128)(2,1)S(1)}, u32[]{:S(2)}, u32[]{:S(2)}) collective-permute-start(bf16[64,2,256]{2,0,1:T(8,128)(2,1)S(1)} %get-tuple-element.26), channel_id=1, source_target_pairs={{2,0},{4,2},{6,4},{8,6},{10,8},{12,10},{14,12},{16,14},{18,16},{20... | collective-permute-start | bytes 196616 | tf_op jit(solution)/shard_map/ppermute | solution.py:18
  81.0 10.3 %collective-permute-start.10 = (bf16[64,36,2]{0,2,1:T(2,128)(2,1)S(1)}, bf16[64,36,2]{0,2,1:T(2,128)(2,1)S(1)}, u32[]{:S(2)}, u32[]{:S(2)}) collective-permute-start(bf16[64,36,2]{0,2,1:T(2,128)(2,1)S(1)} %copy.15), channel_id=1, source_target_pairs={{0,1},{2,3},{4,5},{6,7},{8,9},{10,11},{12,13},{14,15},{16,17},{18,... | collective-permute-start | bytes 27656 | tf_op jit(solution)/shard_map/ppermute | solution.py:17
  82.3 8.7 %collective-permute-start.11 = (bf16[64,36,2]{0,2,1:T(2,128)(2,1)}, bf16[64,36,2]{0,2,1:T(2,128)(2,1)S(1)}, u32[]{:S(2)}, u32[]{:S(2)}) collective-permute-start(bf16[64,36,2]{0,2,1:T(2,128)(2,1)} %copy.17), channel_id=1, source_target_pairs={{1,0},{3,2},{5,4},{7,6},{9,8},{11,10},{13,12},{15,14},{17,16},{19,... | collective-permute-start | bytes 27656 | tf_op jit(solution)/shard_map/ppermute | solution.py:18
  100.6 7.6 %collective-permute-start.12 = (bf16[64,4,256]{2,0,1:T(8,128)(2,1)S(1)}, bf16[64,4,256]{2,0,1:T(8,128)(2,1)S(1)}, u32[]{:S(2)}, u32[]{:S(2)}) collective-permute-start(bf16[64,4,256]{2,0,1:T(8,128)(2,1)S(1)} %get-tuple-element.23), channel_id=1, source_target_pairs={{0,2},{2,4},{4,6},{6,8},{8,10},{10,12},{12,14},{14,16},{16,18},{18... | collective-permute-start | bytes 393224 | tf_op jit(solution)/shard_map/ppermute | solution.py:17
  103.7 7.2 %collective-permute-start.13 = (bf16[64,4,256]{2,0,1:T(8,128)(2,1)S(1)}, bf16[64,4,256]{2,0,1:T(8,128)(2,1)S(1)}, u32[]{:S(2)}, u32[]{:S(2)}) collective-permute-start(bf16[64,4,256]{2,0,1:T(8,128)(2,1)S(1)} %get-tuple-element.24), channel_id=1, source_target_pairs={{2,0},{4,2},{6,4},{8,6},{10,8},{12,10},{14,12},{16,14},{18,16},{20... | collective-permute-start | bytes 393224 | tf_op jit(solution)/shard_map/ppermute | solution.py:18
  114.0 9.6 %collective-permute-start.14 = (bf16[64,40,4]{0,1,2:T(8,128)(2,1)S(1)}, bf16[64,40,4]{0,1,2:T(8,128)(2,1)S(1)}, u32[]{:S(2)}, u32[]{:S(2)}) collective-permute-start(bf16[64,40,4]{0,1,2:T(8,128)(2,1)S(1)} %copy.19), channel_id=1, source_target_pairs={{0,1},{2,3},{4,5},{6,7},{8,9},{10,11},{12,13},{14,15},{16,17},{18,... | collective-permute-start | bytes 61448 | tf_op jit(solution)/shard_map/ppermute | solution.py:17
  115.3 7.9 %collective-permute-start.15 = (bf16[64,40,4]{0,1,2:T(8,128)(2,1)S(1)}, bf16[64,40,4]{0,1,2:T(8,128)(2,1)S(1)}, u32[]{:S(2)}, u32[]{:S(2)}) collective-permute-start(bf16[64,40,4]{0,1,2:T(8,128)(2,1)S(1)} %copy.21), channel_id=1, source_target_pairs={{1,0},{3,2},{5,4},{7,6},{9,8},{11,10},{13,12},{15,14},{17,16},{19,... | collective-permute-start | bytes 61448 | tf_op jit(solution)/shard_map/ppermute | solution.py:18
  133.9 6.9 %collective-permute-start.16 = (bf16[64,8,256]{2,0,1:T(8,128)(2,1)S(1)}, bf16[64,8,256]{2,0,1:T(8,128)(2,1)S(1)}, u32[]{:S(2)}, u32[]{:S(2)}) collective-permute-start(bf16[64,8,256]{2,0,1:T(8,128)(2,1)S(1)} %get-tuple-element.21), channel_id=1, source_target_pairs={{0,2},{2,4},{4,6},{6,8},{8,10},{10,12},{12,14},{14,16},{16,18},{18... | collective-permute-start | bytes 786440 | tf_op jit(solution)/shard_map/ppermute | solution.py:17
  136.3 8.6 %collective-permute-start.17 = (bf16[64,8,256]{2,0,1:T(8,128)(2,1)S(1)}, bf16[64,8,256]{2,0,1:T(8,128)(2,1)S(1)}, u32[]{:S(2)}, u32[]{:S(2)}) collective-permute-start(bf16[64,8,256]{2,0,1:T(8,128)(2,1)S(1)} %get-tuple-element.22), channel_id=1, source_target_pairs={{2,0},{4,2},{6,4},{8,6},{10,8},{12,10},{14,12},{16,14},{18,16},{20... | collective-permute-start | bytes 786440 | tf_op jit(solution)/shard_map/ppermute | solution.py:18
  146.7 9.6 %collective-permute-start.18 = (bf16[64,48,8]{0,2,1:T(8,128)(2,1)S(1)}, bf16[64,48,8]{0,2,1:T(8,128)(2,1)S(1)}, u32[]{:S(2)}, u32[]{:S(2)}) collective-permute-start(bf16[64,48,8]{0,2,1:T(8,128)(2,1)S(1)} %copy.23), channel_id=1, source_target_pairs={{0,1},{2,3},{4,5},{6,7},{8,9},{10,11},{12,13},{14,15},{16,17},{18,... | collective-permute-start | bytes 147464 | tf_op jit(solution)/shard_map/ppermute | solution.py:17
  148.0 7.9 %collective-permute-start.19 = (bf16[64,48,8]{0,2,1:T(8,128)(2,1)}, bf16[64,48,8]{0,2,1:T(8,128)(2,1)S(1)}, u32[]{:S(2)}, u32[]{:S(2)}) collective-permute-start(bf16[64,48,8]{0,2,1:T(8,128)(2,1)} %copy.25), channel_id=1, source_target_pairs={{1,0},{3,2},{5,4},{7,6},{9,8},{11,10},{13,12},{15,14},{17,16},{19,... | collective-permute-start | bytes 147464 | tf_op jit(solution)/shard_map/ppermute | solution.py:18
  (20 other events, 63.9 us)
where the time goes:
time: 167 us; the launch traced here: 166 us
  starting transfers between devices  50.8 us (30%)
  matrix products  48 us (29%)
  local copies, waits for them, and re-layouts  21.6 us (13%)
  waiting for transfers between devices  17.3 us (10%)
  blocking collectives  17 us (10%)
  other arithmetic  10.3 us (6%)
    dot_general x36, matrix products, offset_sum(): jnp.einsum('oc,cij->oij', block, window_extent, preferred_element_type=jn...  44 us
    ppermute x10, starting transfers between devices, padded_2(): after = lax.ppermute(leading, axis, down)  28.7 us
    ppermute x10, starting transfers between devices, padded_2(): before = lax.ppermute(last, axis, up)  22.1 us
    ppermute x10, waiting for transfers between devices, padded_2(): after = lax.ppermute(leading, axis, down)  17.3 us
    all_gather x1, blocking collectives, local(): every_right = lax.all_gather(local_right, 'row', axis=0, tiled=True)  17 us
    concatenate x8, other arithmetic, padded_2(): shard = jnp.concatenate([before, shard, after], axis=dim)  9.12 us
    unnamed x50, local copies, waits for them, and re-layouts  8.47 us
    slice x10, local copies, waits for them, and re-layouts, padded_2(): leading = lax.slice_in_dim(shard, 0, width, axis=dim)  5.72 us
  transfers between devices with their start and end apart: 20, of which 6 were waited for; matrix products, arithmetic and copies ran while one was open for 18% of the time, Pallas kernels for 0%

commit v1 on v0

v1 whole, which is shorter than its diff:
```python
import functools

import jax
import jax.numpy as jnp
from jax import lax
from jax.experimental import pallas as pl
from jax.experimental.pallas import tpu as pltpu
from jax.sharding import PartitionSpec as P

MESH = pl.DeviceIdType.MESH
HALO = 16
F32, BF16 = jnp.float32, jnp.bfloat16


def gather_kernel(n, res_ref, out_ref, buf, send_sem, recv_sem):
    me = lax.axis_index("row")
    barrier = pltpu.get_barrier_semaphore()
    for s in range(1, n):
        pl.semaphore_signal(
            barrier, inc=1, device_id={"row": lax.rem(me + s, n)}, device_id_type=MESH
        )
    pl.semaphore_wait(barrier, n - 1)
    copies = []
    for s in range(1, n):
        copy = pltpu.make_async_remote_copy(
            src_ref=res_ref,
            dst_ref=buf.at[me],
            send_sem=send_sem.at[s],
            recv_sem=recv_sem.at[s],
            device_id={"row": lax.rem(me + s, n)},
            device_id_type=MESH,
        )
        copy.start()
        copies.append(copy)
    for copy in copies:
        copy.wait()
    out_ref[...] = buf[...]
    out_ref[me] = res_ref[...]


def gather_residues(residues, n):
    length = residues.shape[0]
    return pl.pallas_call(
        functools.partial(gather_kernel, n),
        out_shape=jax.ShapeDtypeStruct((n, 1, length), jnp.int32),
        in_specs=[pl.BlockSpec(memory_space=pltpu.VMEM)],
        out_specs=pl.BlockSpec(memory_space=pltpu.VMEM),
        scratch_shapes=[
            pltpu.VMEM((n, 1, length), jnp.int32),
            pltpu.SemaphoreType.DMA((n,)),
            pltpu.SemaphoreType.DMA((n,)),
        ],
        compiler_params=pltpu.CompilerParams(collective_id=0, has_side_effects=True),
        name="gather",
    )(residues.reshape(1, length))


def elu(v):
    return jnp.where(v > 0, v, jnp.exp(jnp.minimum(v, 0.0)) - 1.0)


def main_kernel(
    dims, res_ref, table_ref, w1_ref, w2_ref, prow_ref, pcol_ref, pw_ref, out_ref,
    tab, emb, xs, fs, cols, la, lb, right_ref, pair, act_a, act_b, bw,
):
    rows, ncol, span, tile, chans, kernel, layers = dims
    me_r, me_c = lax.axis_index("row"), lax.axis_index("col")
    window = rows * span
    width = table_ref.shape[1]
    half = kernel // 2
    edge = 2 * HALO
    n_row, n_col = span + 2 * edge, tile + 2 * edge
    height, wide = span + 2 * HALO, tile + 2 * HALO
    two = 2 * chans

    zero = jnp.zeros((chans, chans), BF16)
    for layer in range(layers):
        w = pw_ref[layer]
        blk = lambda ty, tx: w[:, (3 * ty + tx) * chans : (3 * ty + tx + 1) * chans]
        for tx in range(3):
            b0, b1, b2 = (blk(ty, tx) for ty in range(3))
            if layer == 0:
                lines = ([b1, b2, zero, b0], [b0, b1, b2, zero])
            else:
                lines = ([b0, zero, b1, zero, b2, zero], [zero, b0, zero, b1, zero, b2])
            for h in range(2):
                row = jnp.concatenate(lines[h], axis=1)
                bw[layer, pl.ds(tx * two + h * chans, chans), 0 : row.shape[1]] = row

    tab[...] = jnp.zeros_like(tab)
    tab[0 : table_ref.shape[0], :] = table_ref[...]
    emb[0:edge, :] = jnp.zeros((edge, width), F32)
    emb[edge + window : 2 * edge + window, :] = jnp.zeros((edge, width), F32)
    per = 128 // span
    vocab = lax.broadcasted_iota(jnp.int32, (tab.shape[0], 128), 0)
    for g in range(window // 128):
        line = jnp.concatenate([res_ref[per * g + m] for m in range(per)], axis=1)
        hot = (jnp.broadcast_to(line, vocab.shape) == vocab).astype(F32).astype(BF16)
        emb[edge + 128 * g : edge + 128 * (g + 1), :] = lax.dot_general(
            hot, tab[...], (((0,), (0,)), ((), ())), preferred_element_type=F32
        )
    xs[0:n_row, :] = emb[pl.ds(pl.multiple_of(me_r * span, span), n_row), :]
    xs[n_row : n_row + n_col, :] = emb[pl.ds(pl.multiple_of(me_c * tile, tile), n_col), :]

    n_first = n_row + n_col - 2 * half
    n_second = n_first - 2 * half
    for k in range(kernel):
        cols[:, k * width : (k + 1) * width] = xs[k : k + n_first, :].astype(BF16)
    first = elu(jnp.dot(cols[...], w1_ref[...], preferred_element_type=F32))
    at = lax.broadcasted_iota(jnp.int32, (n_first, width), 0) + half
    pos = at + jnp.where(at < n_row, me_r * span - edge, me_c * tile - edge - n_row)
    first = jnp.where((pos >= 0) & (pos < window), first, 0.0)
    fs[...] = first.astype(BF16).astype(F32)
    for k in range(kernel):
        cols[0:n_second, k * width : (k + 1) * width] = fs[k : k + n_second, :].astype(BF16)
    second = elu(jnp.dot(cols[0:n_second, :], w2_ref[...], preferred_element_type=F32))
    second = (fs[half : half + n_second, :] + second).astype(BF16)

    blank = jnp.zeros((width, chans), BF16)
    pr, pc = prow_ref[...], pcol_ref[...]
    s_row, s_col = second[0:height], second[n_row : n_row + wide]
    dot = functools.partial(jnp.dot, preferred_element_type=F32)
    la[...] = dot(s_row, jnp.concatenate([pr, blank], axis=1)).astype(BF16).astype(F32)
    lb[...] = dot(s_row, jnp.concatenate([blank, pr], axis=1)).astype(BF16).astype(F32)
    right_ref[...] = dot(s_col, jnp.concatenate([pc, pc], axis=1)).astype(BF16).astype(F32)
    n_pair = height // 2
    blank_pair = jnp.zeros((wide, two), BF16)
    act_a[0] = blank_pair
    act_a[n_pair + 1] = blank_pair

    def mask(act):
        side = jnp.zeros((HALO // 2, wide, two), BF16)
        stripe = jnp.zeros((n_pair + 2, HALO, two), BF16)

        @pl.when(me_r == 0)
        def _():
            act[1 : 1 + HALO // 2] = side

        @pl.when(me_r == rows - 1)
        def _():
            act[1 + n_pair - HALO // 2 : 1 + n_pair] = side

        @pl.when(me_c == 0)
        def _():
            act[:, 0:HALO, :] = stripe

        @pl.when(me_c == ncol - 1)
        def _():
            act[:, wide - HALO : wide, :] = stripe

    def start(p, _):
        left = la[pl.ds(2 * p, 1), :] + lb[pl.ds(2 * p + 1, 1), :]
        value = (right_ref[...] + left).astype(BF16)
        pair[p] = value
        act_a[p + 1] = elu(value.astype(F32)).astype(BF16)
        return 0

    lax.fori_loop(0, n_pair, start, 0)
    mask(act_a)

    lane = lax.broadcasted_iota(jnp.int32, (wide, two), 1)
    bufs = (act_a, act_b)
    reach = 0
    for layer in range(layers):
        src, dst = bufs[layer % 2], bufs[(layer + 1) % 2]
        d = 2**layer
        reach += d
        last = layer == layers - 1
        lo = HALO // 2 if last else reach // 2
        depth = 4 * chans if layer == 0 else 6 * chans

        def step(p, _, layer=layer, src=src, dst=dst, d=d, last=last, depth=depth):
            if layer == 0:
                outer = jnp.where(lane < chans, src[p + 2], src[p])
                lhs = jnp.concatenate([src[p + 1], outer], axis=1)
            else:
                e = d // 2
                lhs = jnp.concatenate([src[p + 1 - e], src[p + 1], src[p + 1 + e]], axis=1)
            got = lax.dot_general(
                lhs, bw[layer, :, 0:depth], (((1,), (1,)), ((), ())), preferred_element_type=F32
            )
            mid = got[:, two : 2 * two]
            low = pltpu.roll(got[:, 0:two], d, 0)
            high = pltpu.roll(got[:, 2 * two : 3 * two], wide - d, 0)
            value = (pair[p].astype(F32) + (low + mid + high)).astype(BF16)
            if last:
                turned = value[HALO : HALO + tile].astype(F32).T.astype(BF16)
                out_ref[2 * (p - HALO // 2)] = turned[0:chans]
                out_ref[2 * (p - HALO // 2) + 1] = turned[chans:two]
            else:
                pair[p] = value
                dst[p + 1] = elu(value.astype(F32)).astype(BF16)
            return 0

        lax.fori_loop(lo, n_pair - lo, step, 0)
        if not last:
            mask(dst)


def local(residues, embed_table, conv_first, conv_second, proj_row, proj_col, pair_weights):
    rows, ncol = lax.axis_size("row"), lax.axis_size("col")
    span = residues.shape[0]
    window = span * rows
    tile = window // ncol
    width = embed_table.shape[1]
    chans = proj_row.shape[1]
    layers = pair_weights.shape[0]
    kernel = conv_first.shape[0] // width
    half = kernel // 2
    everyone = gather_residues(residues, rows)
    edge = 2 * HALO
    total = span + tile + 4 * edge
    height, wide = span + 2 * HALO, tile + 2 * HALO
    n_pair = height // 2
    two = 2 * chans
    vmem = pl.BlockSpec(memory_space=pltpu.VMEM)
    out = pl.pallas_call(
        functools.partial(main_kernel, (rows, ncol, span, tile, chans, kernel, layers)),
        out_shape=jax.ShapeDtypeStruct((span, chans, tile), BF16),
        in_specs=[vmem] * 7,
        out_specs=vmem,
        scratch_shapes=[
            pltpu.VMEM((32, width), BF16),
            pltpu.VMEM((window + 2 * edge, width), F32),
            pltpu.VMEM((total, width), F32),
            pltpu.VMEM((total - 2 * half, width), F32),
            pltpu.VMEM((total - 2 * half, kernel * width), BF16),
            pltpu.VMEM((height, two), F32),
            pltpu.VMEM((height, two), F32),
            pltpu.VMEM((wide, two), F32),
            pltpu.VMEM((n_pair, wide, two), BF16),
            pltpu.VMEM((n_pair + 2, wide, two), BF16),
            pltpu.VMEM((n_pair + 2, wide, two), BF16),
            pltpu.VMEM((layers, 6 * chans, 6 * chans), BF16),
        ],
        compiler_params=pltpu.CompilerParams(vmem_limit_bytes=48 * 1024 * 1024),
        name="features",
    )(everyone, embed_table, conv_first, conv_second, proj_row, proj_col, pair_weights)
    return jnp.transpose(out, (1, 0, 2))


def solution(mesh):
    return jax.shard_map(
        local,
        mesh=mesh,
        in_specs=(P("row"), P(), P(), P(), P(), P(), P()),
        out_specs=P(None, "row", "col"),
        check_vma=False,
    )
```

time: 167 us -> 60.7 us (0.36)
  the two profiles are of different devices: /device:TPU:7 before, /device:TPU:0 now
where the time goes in v1:
time: 60.7 us; the launch traced here: 60.3 us
  Pallas kernels  51.3 us (85%)
  local copies, waits for them, and re-layouts  8.93 us (15%)
    pallas_call x1, Pallas kernels, local(): pl.pallas_call(functools.partial(main_kernel, (rows, ncol, span, tile, ch...  41.6 us
    pallas_call x1, Pallas kernels, gather_residues(): pl.pallas_call(functools.partial(gather_kernel, n), out_shape=jax.ShapeDt...  9.76 us
    unnamed x12, local copies, waits for them, and re-layouts  7.38 us
    transpose x1, local copies, waits for them, and re-layouts, local(): return jnp.transpose(out, (1, 0, 2))  1.55 us

profile of v1, /device:TPU:0, one launch (start us, length us, event | category | flops | bytes accessed | tf_op | source)
XLA Modules:
  0.0 60.3 jit_solution(12235000471352352361)
XLA Ops:
  0.0 9.8 %gather.1.res_ref = s32[16,1,32]{2,1,0:T(1,128)} custom-call(s32[1,32]{1,0:T(1,128)} %bitcast.3), custom_call_target="tpu_custom_call" | custom-call | tf_op jit(solution)/shard_map/gather/pallas_call | solution.py:43
  9.8 0.9 %copy.8.prow_ref = bf16[256,64]{1,0:T(8,128)(2,1)S(1)} copy(bf16[256,64]{0,1:T(8,128)(2,1)} %param.11) | data formatting | bytes 65536 | tf_op args[4]
  10.6 0.9 %copy.9.pcol_ref = bf16[256,64]{1,0:T(8,128)(2,1)S(1)} copy(bf16[256,64]{0,1:T(8,128)(2,1)} %param.12) | data formatting | bytes 65536 | tf_op args[5]
  11.5 0.0 copy-start
  11.5 1.6 %copy-done = bf16[4352,256]{1,0:T(8,128)(2,1)S(1)} copy-done((bf16[4352,256]{1,0:T(8,128)(2,1)S(1)}, bf16[4352,256]{1,0:T(8,128)(2,1)}, u32[]{:S(2)}) %copy-start) | copy-done | bytes 2228248
  13.2 0.0 copy-start.1
  13.2 1.6 %copy-done.1 = bf16[4352,256]{1,0:T(8,128)(2,1)S(1)} copy-done((bf16[4352,256]{1,0:T(8,128)(2,1)S(1)}, bf16[4352,256]{1,0:T(8,128)(2,1)}, u32[]{:S(2)}) %copy-start.1) | copy-done | bytes 2228248
  14.8 0.0 copy-start.2
  14.8 1.0 %copy-done.2 = bf16[4,64,576]{2,1,0:T(8,128)(2,1)S(1)} copy-done((bf16[4,64,576]{2,1,0:T(8,128)(2,1)S(1)}, bf16[4,64,576]{2,1,0:T(8,128)(2,1)}, u32[]{:S(2)}) %copy-start.2) | copy-done | bytes 294936
  15.8 0.0 copy-start.3
  15.8 0.7 %copy-done.3 = s32[16,1,32]{2,1,0:T(1,128)S(1)} copy-done((s32[16,1,32]{2,1,0:T(1,128)S(1)}, s32[16,1,32]{2,1,0:T(1,128)}, u32[]{:S(2)}) %copy-start.3) | copy-done | bytes 2072
  16.5 0.0 copy-start.4
  16.5 0.7 %copy-done.4 = bf16[21,256]{1,0:T(8,128)(2,1)S(1)} copy-done((bf16[21,256]{1,0:T(8,128)(2,1)S(1)}, bf16[21,256]{1,0:T(8,128)(2,1)}, u32[]{:S(2)}) %copy-start.4) | copy-done | bytes 10776
  17.2 41.6 %features.1 = bf16[32,64,256]{2,1,0:T(8,128)(2,1)S(1)} custom-call(s32[16,1,32]{2,1,0:T(1,128)S(1)} %copy-done.3, bf16[21,256]{1,0:T(8,128)(2,1)S(1)} %copy-done.4, bf16[4352,256]{1,0:T(8,128)(2,1)S(1)} %copy-done, bf16[4352,256]{1,0:T(8,128)(2,1)S(1)} %copy-done.1, bf16[256,64]{1,0:T(8,128)(2,1)S(1)} %copy.8.prow_ref, bf16[256,64]{1,0:T(8,128)(2,1)S(1)} %copy.9.pcol_ref, ...), custom_call_target="tpu_custom_call" | custom-call | tf_op jit(solution)/shard_map/features/pallas_call | solution.py:217
  58.7 1.6 %copy.10 = bf16[64,32,256]{2,1,0:T(8,128)(2,1)} copy(bf16[64,32,256]{2,0,1:T(8,128)(2,1)S(1)} %bitcast.2) | data formatting | bytes 2097152 | tf_op jit(solution)/shard_map/transpose | solution.py:239
Async XLA Ops:
  11.5 1.6 %copy-start = (bf16[4352,256]{1,0:T(8,128)(2,1)S(1)}, bf16[4352,256]{1,0:T(8,128)(2,1)}, u32[]{:S(2)}) copy-start(bf16[4352,256]{1,0:T(8,128)(2,1)} %w1_ref.1) | copy-start | bytes 6684676
  13.2 1.6 %copy-start.1 = (bf16[4352,256]{1,0:T(8,128)(2,1)S(1)}, bf16[4352,256]{1,0:T(8,128)(2,1)}, u32[]{:S(2)}) copy-start(bf16[4352,256]{1,0:T(8,128)(2,1)} %w2_ref.1) | copy-start | bytes 6684676
  14.8 1.0 %copy-start.2 = (bf16[4,64,576]{2,1,0:T(8,128)(2,1)S(1)}, bf16[4,64,576]{2,1,0:T(8,128)(2,1)}, u32[]{:S(2)}) copy-start(bf16[4,64,576]{2,1,0:T(8,128)(2,1)} %pw_ref.1) | copy-start | bytes 884740
  15.8 0.7 %copy-start.3 = (s32[16,1,32]{2,1,0:T(1,128)S(1)}, s32[16,1,32]{2,1,0:T(1,128)}, u32[]{:S(2)}) copy-start(s32[16,1,32]{2,1,0:T(1,128)} %gather.1.res_ref) | copy-start | bytes 6148
  16.5 0.7 %copy-start.4 = (bf16[21,256]{1,0:T(8,128)(2,1)S(1)}, bf16[21,256]{1,0:T(8,128)(2,1)}, u32[]{:S(2)}) copy-start(bf16[21,256]{1,0:T(8,128)(2,1)} %table_ref.1) | copy-start | bytes 32260

commit v2 on v1

--- a/solution.py
+++ b/solution.py
@@ -8,6 +8,8 @@
 from jax.sharding import PartitionSpec as P
 
 MESH = pl.DeviceIdType.MESH
+UNROLL = 4
+PAD = 4
 HALO = 16
 F32, BF16 = jnp.float32, jnp.bfloat16
 
@@ -60,8 +62,8 @@
 
 
 def main_kernel(
-    dims, res_ref, table_ref, w1_ref, w2_ref, prow_ref, pcol_ref, pw_ref, out_ref,
-    tab, emb, xs, fs, cols, la, lb, right_ref, pair, act_a, act_b, bw,
+    dims, res_hbm, table_hbm, w1_hbm, w2_hbm, prow_hbm, pcol_hbm, pw_hbm, out_ref,
+    res_ref, table_ref, w1_ref, w2_ref, prow_ref, pcol_ref, pw_ref, sems, tab, emb, xs, fs, cols, la, lb, right_ref, pair, act_a, act_b, bw,
 ):
     rows, ncol, span, tile, chans, kernel, layers = dims
     me_r, me_c = lax.axis_index("row"), lax.axis_index("col")
@@ -73,20 +75,30 @@
     height, wide = span + 2 * HALO, tile + 2 * HALO
     two = 2 * chans
 
+    pairs = (
+        (pw_hbm, pw_ref), (res_hbm, res_ref), (table_hbm, table_ref), (w1_hbm, w1_ref),
+        (w2_hbm, w2_ref), (prow_hbm, prow_ref), (pcol_hbm, pcol_ref),
+    )
+    loads = [pltpu.make_async_copy(a, b, sems.at[i]) for i, (a, b) in enumerate(pairs)]
+    for load in loads:
+        load.start()
+    loads[0].wait()
+
     zero = jnp.zeros((chans, chans), BF16)
     for layer in range(layers):
-        w = pw_ref[layer]
-        blk = lambda ty, tx: w[:, (3 * ty + tx) * chans : (3 * ty + tx + 1) * chans]
-        for tx in range(3):
-            b0, b1, b2 = (blk(ty, tx) for ty in range(3))
-            if layer == 0:
-                lines = ([b1, b2, zero, b0], [b0, b1, b2, zero])
-            else:
-                lines = ([b0, zero, b1, zero, b2, zero], [zero, b0, zero, b1, zero, b2])
-            for h in range(2):
-                row = jnp.concatenate(lines[h], axis=1)
-                bw[layer, pl.ds(tx * two + h * chans, chans), 0 : row.shape[1]] = row
-
+        w = pw_ref[layer].astype(F32).T.astype(BF16)
+        for g, offset in enumerate((0, 1, 2, -1)):
+            line = []
+            for tx in range(3):
+                for h in range(2):
+                    ty = offset - h + 1
+                    tap = 3 * ty + tx
+                    here = 0 <= ty <= 2
+                    line.append(w[tap * chans : (tap + 1) * chans] if here else zero)
+            bw[layer, g * chans : (g + 1) * chans, :] = jnp.concatenate(line, axis=1)
+
+    loads[1].wait()
+    loads[2].wait()
     tab[...] = jnp.zeros_like(tab)
     tab[0 : table_ref.shape[0], :] = table_ref[...]
     emb[0:edge, :] = jnp.zeros((edge, width), F32)
@@ -106,6 +118,7 @@
     n_second = n_first - 2 * half
     for k in range(kernel):
         cols[:, k * width : (k + 1) * width] = xs[k : k + n_first, :].astype(BF16)
+    loads[3].wait()
     first = elu(jnp.dot(cols[...], w1_ref[...], preferred_element_type=F32))
     at = lax.broadcasted_iota(jnp.int32, (n_first, width), 0) + half
     pos = at + jnp.where(at < n_row, me_r * span - edge, me_c * tile - edge - n_row)
@@ -113,32 +126,42 @@
     fs[...] = first.astype(BF16).astype(F32)
     for k in range(kernel):
         cols[0:n_second, k * width : (k + 1) * width] = fs[k : k + n_second, :].astype(BF16)
+    loads[4].wait()
     second = elu(jnp.dot(cols[0:n_second, :], w2_ref[...], preferred_element_type=F32))
     second = (fs[half : half + n_second, :] + second).astype(BF16)
 
-    blank = jnp.zeros((width, chans), BF16)
+    loads[5].wait()
+    loads[6].wait()
+    blank = jnp.zeros((chans, width), BF16)
     pr, pc = prow_ref[...], pcol_ref[...]
     s_row, s_col = second[0:height], second[n_row : n_row + wide]
     dot = functools.partial(jnp.dot, preferred_element_type=F32)
-    la[...] = dot(s_row, jnp.concatenate([pr, blank], axis=1)).astype(BF16).astype(F32)
-    lb[...] = dot(s_row, jnp.concatenate([blank, pr], axis=1)).astype(BF16).astype(F32)
-    right_ref[...] = dot(s_col, jnp.concatenate([pc, pc], axis=1)).astype(BF16).astype(F32)
+
+    def project(x, *parts):
+        w = jnp.concatenate(parts, axis=0)
+        y = lax.dot_general(x, w, (((1,), (1,)), ((), ())), preferred_element_type=F32)
+        return y.astype(BF16).astype(F32)
+
+    la[...] = project(s_row, pr, blank)
+    lb[...] = project(s_row, blank, pr)
+    right_ref[...] = project(s_col, pc, pc)
     n_pair = height // 2
-    blank_pair = jnp.zeros((wide, two), BF16)
-    act_a[0] = blank_pair
-    act_a[n_pair + 1] = blank_pair
+    blank_pair = jnp.zeros((PAD, wide, two), BF16)
+    for act in (act_a, act_b):
+        act[0:PAD] = blank_pair
+        act[PAD + n_pair : 2 * PAD + n_pair] = blank_pair
 
     def mask(act):
         side = jnp.zeros((HALO // 2, wide, two), BF16)
-        stripe = jnp.zeros((n_pair + 2, HALO, two), BF16)
+        stripe = jnp.zeros((n_pair + 2 * PAD, HALO, two), BF16)
 
         @pl.when(me_r == 0)
         def _():
-            act[1 : 1 + HALO // 2] = side
+            act[PAD : PAD + HALO // 2] = side
 
         @pl.when(me_r == rows - 1)
         def _():
-            act[1 + n_pair - HALO // 2 : 1 + n_pair] = side
+            act[PAD + n_pair - HALO // 2 : PAD + n_pair] = side
 
         @pl.when(me_c == 0)
         def _():
@@ -152,47 +175,67 @@
         left = la[pl.ds(2 * p, 1), :] + lb[pl.ds(2 * p + 1, 1), :]
         value = (right_ref[...] + left).astype(BF16)
         pair[p] = value
-        act_a[p + 1] = elu(value.astype(F32)).astype(BF16)
+        act_a[p + PAD] = elu(value.astype(F32)).astype(BF16)
         return 0
 
     lax.fori_loop(0, n_pair, start, 0)
     mask(act_a)
 
-    lane = lax.broadcasted_iota(jnp.int32, (wide, two), 1)
+    low_half = lax.broadcasted_iota(jnp.int32, (wide, two), 1) < chans
     bufs = (act_a, act_b)
-    reach = 0
     for layer in range(layers):
         src, dst = bufs[layer % 2], bufs[(layer + 1) % 2]
         d = 2**layer
-        reach += d
         last = layer == layers - 1
-        lo = HALO // 2 if last else reach // 2
-        depth = 4 * chans if layer == 0 else 6 * chans
-
-        def step(p, _, layer=layer, src=src, dst=dst, d=d, last=last, depth=depth):
-            if layer == 0:
-                outer = jnp.where(lane < chans, src[p + 2], src[p])
-                lhs = jnp.concatenate([src[p + 1], outer], axis=1)
+
+        def step(q, _, layer=layer, src=src, dst=dst, d=d, last=last):
+            if last:
+                slots = [HALO // 2 + 2 * q, HALO // 2 + 2 * q + 1]
             else:
-                e = d // 2
-                lhs = jnp.concatenate([src[p + 1 - e], src[p + 1], src[p + 1 + e]], axis=1)
-            got = lax.dot_general(
-                lhs, bw[layer, :, 0:depth], (((1,), (1,)), ((), ())), preferred_element_type=F32
+                x = 2 * d * lax.div(q, d) + lax.rem(q, d)
+                slots = [x, x + d]
+            lhs = jnp.concatenate(
+                [
+                    jnp.concatenate(
+                        [
+                            src[p + PAD],
+                            jnp.where(low_half, src[p + PAD + d], src[p + PAD - d]),
+                        ],
+                        axis=1,
+                    )
+                    for p in slots
+                ],
+                axis=0,
             )
+            got = dot(lhs, bw[layer])
+            low = pltpu.roll(got[:, 0:two], d, 0)
             mid = got[:, two : 2 * two]
-            low = pltpu.roll(got[:, 0:two], d, 0)
-            high = pltpu.roll(got[:, 2 * two : 3 * two], wide - d, 0)
-            value = (pair[p].astype(F32) + (low + mid + high)).astype(BF16)
+            high = pltpu.roll(got[:, 2 * two : 3 * two], 2 * wide - d, 0)
+            total = low + mid + high
+            values = [
+                pair[p].astype(F32) + total[k * wide : (k + 1) * wide]
+                for k, p in enumerate(slots)
+            ]
             if last:
-                turned = value[HALO : HALO + tile].astype(F32).T.astype(BF16)
-                out_ref[2 * (p - HALO // 2)] = turned[0:chans]
-                out_ref[2 * (p - HALO // 2) + 1] = turned[chans:two]
+                for p, value in zip(slots, values):
+                    turned = value[HALO : HALO + tile].T.astype(BF16)
+                    at = p - HALO // 2
+                    line = 2 * d * lax.div(at, d) + lax.rem(at, d)
+                    out_ref[line] = turned[0:chans]
+                    out_ref[line + d] = turned[chans:two]
             else:
-                pair[p] = value
-                dst[p + 1] = elu(value.astype(F32)).astype(BF16)
+                one, other = (v.astype(BF16) for v in values)
+                new = [
+                    jnp.where(low_half, one, pltpu.roll(other, chans, 1)),
+                    jnp.where(low_half, pltpu.roll(one, chans, 1), other),
+                ]
+                for p, value in zip(slots, new):
+                    pair[p] = value
+                    dst[p + PAD] = elu(value.astype(F32)).astype(BF16)
             return 0
 
-        lax.fori_loop(lo, n_pair - lo, step, 0)
+        steps = (n_pair - HALO) // 2 if last else n_pair // 2
+        lax.fori_loop(0, steps, step, 0, unroll=UNROLL)
         if not last:
             mask(dst)
 
@@ -217,9 +260,17 @@
     out = pl.pallas_call(
         functools.partial(main_kernel, (rows, ncol, span, tile, chans, kernel, layers)),
         out_shape=jax.ShapeDtypeStruct((span, chans, tile), BF16),
-        in_specs=[vmem] * 7,
+        in_specs=[pl.BlockSpec(memory_space=pltpu.HBM)] * 7,
         out_specs=vmem,
         scratch_shapes=[
+            pltpu.VMEM(everyone.shape, jnp.int32),
+            pltpu.VMEM(embed_table.shape, BF16),
+            pltpu.VMEM(conv_first.shape, BF16),
+            pltpu.VMEM(conv_second.shape, BF16),
+            pltpu.VMEM((chans, width), BF16),
+            pltpu.VMEM((chans, width), BF16),
+            pltpu.VMEM(pair_weights.shape, BF16),
+            pltpu.SemaphoreType.DMA((7,)),
             pltpu.VMEM((32, width), BF16),
             pltpu.VMEM((window + 2 * edge, width), F32),
             pltpu.VMEM((total, width), F32),
@@ -229,13 +280,13 @@
             pltpu.VMEM((height, two), F32),
             pltpu.VMEM((wide, two), F32),
             pltpu.VMEM((n_pair, wide, two), BF16),
-            pltpu.VMEM((n_pair + 2, wide, two), BF16),
-            pltpu.VMEM((n_pair + 2, wide, two), BF16),
-            pltpu.VMEM((layers, 6 * chans, 6 * chans), BF16),
+            pltpu.VMEM((n_pair + 2 * PAD, wide, two), BF16),
+            pltpu.VMEM((n_pair + 2 * PAD, wide, two), BF16),
+            pltpu.VMEM((layers, 4 * chans, 6 * chans), BF16),
         ],
-        compiler_params=pltpu.CompilerParams(vmem_limit_bytes=48 * 1024 * 1024),
+        compiler_params=pltpu.CompilerParams(vmem_limit_bytes=60 * 1024 * 1024),
         name="features",
-    )(everyone, embed_table, conv_first, conv_second, proj_row, proj_col, pair_weights)
+    )(everyone, embed_table, conv_first, conv_second, proj_row.T, proj_col.T, pair_weights)
     return jnp.transpose(out, (1, 0, 2))
 
 

time: 60.7 us -> 36.8 us (0.61)
  Pallas kernels: 51.3 us -> 33.8 us
  local copies, waits for them, and re-layouts: 8.93 us -> 2.78 us
    pallas_call x1, Pallas kernels: 41.6 us -> 24.1 us  [local(): pl.pallas_call(functools.partial(main_kernel, (rows, ncol, span, tile, ch...]
    unnamed x12 -> x0, local copies, waits for them, and re-layouts: 7.38 us -> none
    transpose x1, local copies, waits for them, and re-layouts: 1.55 us -> 2.78 us  [local(): return jnp.transpose(out, (1, 0, 2))]
where the time goes in v2:
time: 36.8 us; the launch traced here: 36.6 us
  Pallas kernels  33.8 us (92%)
  local copies, waits for them, and re-layouts  2.78 us (8%)
    pallas_call x1, Pallas kernels, local(): pl.pallas_call(functools.partial(main_kernel, (rows, ncol, span, tile, ch...  24.1 us
    pallas_call x1, Pallas kernels, gather_residues(): pl.pallas_call(functools.partial(gather_kernel, n), out_shape=jax.ShapeDt...  9.75 us
    transpose x1, local copies, waits for them, and re-layouts, local(): return jnp.transpose(out, (1, 0, 2))  2.78 us

profile of v2, /device:TPU:0, one launch (start us, length us, event | category | flops | bytes accessed | tf_op | source)
XLA Modules:
  0.0 36.6 jit_solution(14969438646594080491)
XLA Ops:
  0.0 9.8 %gather.1.res_hbm = s32[16,1,32]{2,1,0:T(1,128)} custom-call(s32[1,32]{1,0:T(1,128)} %bitcast.7), custom_call_target="tpu_custom_call" | custom-call | tf_op jit(solution)/shard_map/gather/pallas_call | solution.py:45
  9.8 24.1 %features.1 = bf16[32,64,256]{2,1,0:T(8,128)(2,1)} custom-call(s32[16,1,32]{2,1,0:T(1,128)} %gather.1.res_hbm, bf16[21,256]{1,0:T(8,128)(2,1)} %table_hbm.1, bf16[4352,256]{1,0:T(8,128)(2,1)} %w1_hbm.1, bf16[4352,256]{1,0:T(8,128)(2,1)} %w2_hbm.1, bf16[64,256]{1,0:T(8,128)(2,1)} %bitcast.5, bf16[64,256]{1,0:T(8,128)(2,1)} %bitcast.6, bf16[4,64,576]{2,1,0:T(8,128)(2,1)} %pw_hbm.1), custom_call_target="tpu_custom_call" | custom-call | tf_op jit(solution)/shard_map/features/pallas_call | solution.py:260
  33.8 2.8 %copy.8 = bf16[64,32,256]{2,1,0:T(8,128)(2,1)} copy(bf16[64,32,256]{2,0,1:T(8,128)(2,1)} %bitcast.4) | data formatting | bytes 2097152 | tf_op jit(solution)/shard_map/transpose | solution.py:290

commit v3 on v2

--- a/solution.py
+++ b/solution.py
@@ -8,62 +8,19 @@
 from jax.sharding import PartitionSpec as P
 
 MESH = pl.DeviceIdType.MESH
-UNROLL = 4
+UNROLL = 8
 PAD = 4
 HALO = 16
 F32, BF16 = jnp.float32, jnp.bfloat16
 
 
-def gather_kernel(n, res_ref, out_ref, buf, send_sem, recv_sem):
-    me = lax.axis_index("row")
-    barrier = pltpu.get_barrier_semaphore()
-    for s in range(1, n):
-        pl.semaphore_signal(
-            barrier, inc=1, device_id={"row": lax.rem(me + s, n)}, device_id_type=MESH
-        )
-    pl.semaphore_wait(barrier, n - 1)
-    copies = []
-    for s in range(1, n):
-        copy = pltpu.make_async_remote_copy(
-            src_ref=res_ref,
-            dst_ref=buf.at[me],
-            send_sem=send_sem.at[s],
-            recv_sem=recv_sem.at[s],
-            device_id={"row": lax.rem(me + s, n)},
-            device_id_type=MESH,
-        )
-        copy.start()
-        copies.append(copy)
-    for copy in copies:
-        copy.wait()
-    out_ref[...] = buf[...]
-    out_ref[me] = res_ref[...]
-
-
-def gather_residues(residues, n):
-    length = residues.shape[0]
-    return pl.pallas_call(
-        functools.partial(gather_kernel, n),
-        out_shape=jax.ShapeDtypeStruct((n, 1, length), jnp.int32),
-        in_specs=[pl.BlockSpec(memory_space=pltpu.VMEM)],
-        out_specs=pl.BlockSpec(memory_space=pltpu.VMEM),
-        scratch_shapes=[
-            pltpu.VMEM((n, 1, length), jnp.int32),
-            pltpu.SemaphoreType.DMA((n,)),
-            pltpu.SemaphoreType.DMA((n,)),
-        ],
-        compiler_params=pltpu.CompilerParams(collective_id=0, has_side_effects=True),
-        name="gather",
-    )(residues.reshape(1, length))
-
-
 def elu(v):
     return jnp.where(v > 0, v, jnp.exp(jnp.minimum(v, 0.0)) - 1.0)
 
 
 def main_kernel(
     dims, res_hbm, table_hbm, w1_hbm, w2_hbm, prow_hbm, pcol_hbm, pw_hbm, out_ref,
-    res_ref, table_ref, w1_ref, w2_ref, prow_ref, pcol_ref, pw_ref, sems, tab, emb, xs, fs, cols, la, lb, right_ref, pair, act_a, act_b, bw,
+    res_ref, table_ref, w1_ref, w2_ref, prow_ref, pcol_ref, pw_ref, sems, send_sem, recv_sem, tab, emb, xs, fs, cols, la, lb, right_ref, pair, act_a, act_b, bw,
 ):
     rows, ncol, span, tile, chans, kernel, layers = dims
     me_r, me_c = lax.axis_index("row"), lax.axis_index("col")
@@ -75,8 +32,13 @@
     height, wide = span + 2 * HALO, tile + 2 * HALO
     two = 2 * chans
 
+    barrier = pltpu.get_barrier_semaphore()
+    for k in range(1, rows):
+        pl.semaphore_signal(
+            barrier, inc=1, device_id={"row": lax.rem(me_r + k, rows)}, device_id_type=MESH
+        )
     pairs = (
-        (pw_hbm, pw_ref), (res_hbm, res_ref), (table_hbm, table_ref), (w1_hbm, w1_ref),
+        (pw_hbm, pw_ref), (res_hbm, res_ref.at[me_r]), (table_hbm, table_ref), (w1_hbm, w1_ref),
         (w2_hbm, w2_ref), (prow_hbm, prow_ref), (pcol_hbm, pcol_ref),
     )
     loads = [pltpu.make_async_copy(a, b, sems.at[i]) for i, (a, b) in enumerate(pairs)]
@@ -96,13 +58,35 @@
                     here = 0 <= ty <= 2
                     line.append(w[tap * chans : (tap + 1) * chans] if here else zero)
             bw[layer, g * chans : (g + 1) * chans, :] = jnp.concatenate(line, axis=1)
-
-    loads[1].wait()
+    n_pair = height // 2
+    blank_pair = jnp.zeros((PAD, wide, two), BF16)
+    for act in (act_a, act_b):
+        act[0:PAD] = blank_pair
+        act[PAD + n_pair : 2 * PAD + n_pair] = blank_pair
+
+    pl.semaphore_wait(barrier, rows - 1)
+    copies = [
+        pltpu.make_async_remote_copy(
+            src_ref=res_hbm,
+            dst_ref=res_ref.at[me_r],
+            send_sem=send_sem.at[k],
+            recv_sem=recv_sem.at[k],
+            device_id={"row": lax.rem(me_r + k, rows)},
+            device_id_type=MESH,
+        )
+        for k in range(1, rows)
+    ]
+    for copy in copies:
+        copy.start()
+
     loads[2].wait()
     tab[...] = jnp.zeros_like(tab)
     tab[0 : table_ref.shape[0], :] = table_ref[...]
     emb[0:edge, :] = jnp.zeros((edge, width), F32)
     emb[edge + window : 2 * edge + window, :] = jnp.zeros((edge, width), F32)
+    loads[1].wait()
+    for copy in copies:
+        copy.wait()
     per = 128 // span
     vocab = lax.broadcasted_iota(jnp.int32, (tab.shape[0], 128), 0)
     for g in range(window // 128):
@@ -145,11 +129,6 @@
     la[...] = project(s_row, pr, blank)
     lb[...] = project(s_row, blank, pr)
     right_ref[...] = project(s_col, pc, pc)
-    n_pair = height // 2
-    blank_pair = jnp.zeros((PAD, wide, two), BF16)
-    for act in (act_a, act_b):
-        act[0:PAD] = blank_pair
-        act[PAD + n_pair : 2 * PAD + n_pair] = blank_pair
 
     def mask(act):
         side = jnp.zeros((HALO // 2, wide, two), BF16)
@@ -250,7 +229,6 @@
     layers = pair_weights.shape[0]
     kernel = conv_first.shape[0] // width
     half = kernel // 2
-    everyone = gather_residues(residues, rows)
     edge = 2 * HALO
     total = span + tile + 4 * edge
     height, wide = span + 2 * HALO, tile + 2 * HALO
@@ -263,7 +241,7 @@
         in_specs=[pl.BlockSpec(memory_space=pltpu.HBM)] * 7,
         out_specs=vmem,
         scratch_shapes=[
-            pltpu.VMEM(everyone.shape, jnp.int32),
+            pltpu.VMEM((rows, 1, span), jnp.int32),
             pltpu.VMEM(embed_table.shape, BF16),
             pltpu.VMEM(conv_first.shape, BF16),
             pltpu.VMEM(conv_second.shape, BF16),
@@ -271,6 +249,8 @@
             pltpu.VMEM((chans, width), BF16),
             pltpu.VMEM(pair_weights.shape, BF16),
             pltpu.SemaphoreType.DMA((7,)),
+            pltpu.SemaphoreType.DMA((rows,)),
+            pltpu.SemaphoreType.DMA((rows,)),
             pltpu.VMEM((32, width), BF16),
             pltpu.VMEM((window + 2 * edge, width), F32),
             pltpu.VMEM((total, width), F32),
@@ -284,9 +264,11 @@
             pltpu.VMEM((n_pair + 2 * PAD, wide, two), BF16),
             pltpu.VMEM((layers, 4 * chans, 6 * chans), BF16),
         ],
-        compiler_params=pltpu.CompilerParams(vmem_limit_bytes=60 * 1024 * 1024),
-        name="features",
-    )(everyone, embed_table, conv_first, conv_second, proj_row.T, proj_col.T, pair_weights)
+        compiler_params=pltpu.CompilerParams(
+            vmem_limit_bytes=60 * 1024 * 1024, collective_id=0, has_side_effects=True
+        ),
+        name="all",
+    )(residues.reshape(1, span), embed_table, conv_first, conv_second, proj_row.T, proj_col.T, pair_weights)
     return jnp.transpose(out, (1, 0, 2))
 
 

time: 36.8 us -> 34.3 us (0.932)
  Pallas kernels: 33.8 us -> 31.4 us
    pallas_call x1 -> x0, Pallas kernels: 9.75 us -> none  [gather_residues(): pl.pallas_call(functools.partial(gather_kernel, n), out_shape=jax.ShapeDt...]
    pallas_call x1, Pallas kernels: 24.1 us -> 31.4 us  [local(): pl.pallas_call(functools.partial(main_kernel, (rows, ncol, span, tile, ch...]
where the time goes in v3:
time: 34.3 us; the launch traced here: 34.1 us
  Pallas kernels  31.4 us (92%)
  local copies, waits for them, and re-layouts  2.78 us (8%)
    pallas_call x1, Pallas kernels, local(): pl.pallas_call(functools.partial(main_kernel, (rows, ncol, span, tile, ch...  31.4 us
    transpose x1, local copies, waits for them, and re-layouts, local(): return jnp.transpose(out, (1, 0, 2))  2.78 us

profile of v3, /device:TPU:0, one launch (start us, length us, event | category | flops | bytes accessed | tf_op | source)
XLA Modules:
  0.0 34.1 jit_solution(7678496839262981898)
XLA Ops:
  0.0 31.4 %all.1 = bf16[32,64,256]{2,1,0:T(8,128)(2,1)} custom-call(s32[1,32]{1,0:T(1,128)} %bitcast.7, bf16[21,256]{1,0:T(8,128)(2,1)} %table_hbm.1, bf16[4352,256]{1,0:T(8,128)(2,1)} %w1_hbm.1, bf16[4352,256]{1,0:T(8,128)(2,1)} %w2_hbm.1, bf16[64,256]{1,0:T(8,128)(2,1)} %bitcast.5, bf16[64,256]{1,0:T(8,128)(2,1)} %bitcast.6, bf16[4,64,576]{2,1,0:T(8,128)(2,1)} %pw_hbm.1), custom_call_target="tpu_custom_call" | custom-call | tf_op jit(solution)/shard_map/all/pallas_call | solution.py:238
  31.4 2.8 %copy.8 = bf16[64,32,256]{2,1,0:T(8,128)(2,1)} copy(bf16[64,32,256]{2,0,1:T(8,128)(2,1)} %bitcast.4) | data formatting | bytes 2097152 | tf_op jit(solution)/shard_map/transpose | solution.py:272

commit v4 on v3

--- a/solution.py
+++ b/solution.py
@@ -157,7 +157,7 @@
         act_a[p + PAD] = elu(value.astype(F32)).astype(BF16)
         return 0
 
-    lax.fori_loop(0, n_pair, start, 0)
+    lax.fori_loop(0, n_pair, start, 0, unroll=4)
     mask(act_a)
 
     low_half = lax.broadcasted_iota(jnp.int32, (wide, two), 1) < chans
@@ -167,9 +167,11 @@
         d = 2**layer
         last = layer == layers - 1
 
-        def step(q, _, layer=layer, src=src, dst=dst, d=d, last=last):
+        def step(q, _, layer=layer, src=src, dst=dst, d=d, last=last, rim=False):
             if last:
                 slots = [HALO // 2 + 2 * q, HALO // 2 + 2 * q + 1]
+            elif rim:
+                slots = [q + d, n_pair - 2 * d + q]
             else:
                 x = 2 * d * lax.div(q, d) + lax.rem(q, d)
                 slots = [x, x + d]
@@ -204,17 +206,28 @@
                     out_ref[line + d] = turned[chans:two]
             else:
                 one, other = (v.astype(BF16) for v in values)
-                new = [
-                    jnp.where(low_half, one, pltpu.roll(other, chans, 1)),
-                    jnp.where(low_half, pltpu.roll(one, chans, 1), other),
-                ]
+                if rim:
+                    first_pair, last_pair = one, other
+                    new = [
+                        pltpu.roll(first_pair, chans, 1), first_pair,
+                        last_pair, pltpu.roll(last_pair, chans, 1),
+                    ]
+                    slots = [q, q + d, n_pair - 2 * d + q, n_pair - d + q]
+                else:
+                    new = [
+                        jnp.where(low_half, one, pltpu.roll(other, chans, 1)),
+                        jnp.where(low_half, pltpu.roll(one, chans, 1), other),
+                    ]
                 for p, value in zip(slots, new):
                     pair[p] = value
                     dst[p + PAD] = elu(value.astype(F32)).astype(BF16)
             return 0
 
-        steps = (n_pair - HALO) // 2 if last else n_pair // 2
-        lax.fori_loop(0, steps, step, 0, unroll=UNROLL)
+        if last:
+            lax.fori_loop(0, (n_pair - HALO) // 2, step, 0, unroll=UNROLL)
+        else:
+            lax.fori_loop(0, d, functools.partial(step, rim=True), 0, unroll=d)
+            lax.fori_loop(d, n_pair // 2 - d, step, 0, unroll=UNROLL)
         if not last:
             mask(dst)
 

time: 34.3 us -> 33.3 us (0.971)
  Pallas kernels: 31.4 us -> 30.4 us
    pallas_call x1, Pallas kernels: 31.4 us -> 30.4 us  [local(): pl.pallas_call(functools.partial(main_kernel, (rows, ncol, span, tile, ch...]
where the time goes in v4:
time: 33.3 us; the launch traced here: 33.2 us
  Pallas kernels  30.4 us (91%)
  local copies, waits for them, and re-layouts  2.78 us (8%)
    pallas_call x1, Pallas kernels, local(): pl.pallas_call(functools.partial(main_kernel, (rows, ncol, span, tile, ch...  30.4 us
    transpose x1, local copies, waits for them, and re-layouts, local(): return jnp.transpose(out, (1, 0, 2))  2.78 us

profile of v4, /device:TPU:0, one launch (start us, length us, event | category | flops | bytes accessed | tf_op | source)
XLA Modules:
  0.0 33.2 jit_solution(9481497825893382389)
XLA Ops:
  0.0 30.4 %all.1 = bf16[32,64,256]{2,1,0:T(8,128)(2,1)} custom-call(s32[1,32]{1,0:T(1,128)} %bitcast.7, bf16[21,256]{1,0:T(8,128)(2,1)} %table_hbm.1, bf16[4352,256]{1,0:T(8,128)(2,1)} %w1_hbm.1, bf16[4352,256]{1,0:T(8,128)(2,1)} %w2_hbm.1, bf16[64,256]{1,0:T(8,128)(2,1)} %bitcast.5, bf16[64,256]{1,0:T(8,128)(2,1)} %bitcast.6, bf16[4,64,576]{2,1,0:T(8,128)(2,1)} %pw_hbm.1), custom_call_target="tpu_custom_call" | custom-call | tf_op jit(solution)/shard_map/all/pallas_call | solution.py:251
  30.4 2.8 %copy.8 = bf16[64,32,256]{2,1,0:T(8,128)(2,1)} copy(bf16[64,32,256]{2,0,1:T(8,128)(2,1)} %bitcast.4) | data formatting | bytes 2097152 | tf_op jit(solution)/shard_map/transpose | solution.py:285
